TPU v7x, 32 devices: a whole 2x2x4 slice. The times are simulated.
32 devices in a mesh: rep: 16 (over z, y, x), shard: 2 (over core).
Axes of the slice: x: 2, y: 2, z: 4, core: 2. Of those that a mesh axis runs over, the one named last changes fastest.
Arguments:
- grad_parts: float32 [16, 2, 2, 1024, 512], P('rep', 'shard'), may hold values from -6 to 6
- weights: bfloat16 [2, 1024, 512], P(None, 'shard'), may hold values from -3 to 3
- stat_left: float32 [2, 1024, 1024], P(None, 'shard'), may hold values from -12 to 332, as said below
- stat_right: float32 [512, 512], replicated, may hold values from -12 to 238.27417, as said below
- basis_left: bfloat16 [2, 1024, 1024], P(None, 'shard'), may hold values from -0.1875 to 0.1875
- basis_right: bfloat16 [512, 512], replicated, may hold values from -0.25 to 0.25
- moment_first: float32 [2, 1024, 512], P(None, 'shard'), may hold values from -2 to 2
- moment_second: float32 [2, 1024, 512], P(None, 'shard'), may hold values from 0.05 to 1
Outputs:
- weights_new: bfloat16 [2, 1024, 512], replicated
- basis_left_new: bfloat16 [2, 1024, 1024], P(None, 'shard')
- basis_right_new: bfloat16 [512, 512], replicated
- moment_first_new: float32 [2, 1024, 512], P(None, 'shard')
- moment_second_new: float32 [2, 1024, 512], P(None, 'shard')
Inputs may be any that keep to these rules, and one draw needn't show every extreme that they name: `stat_left`: each block is a symmetric matrix. `stat_right`: a symmetric matrix.
All inputs are finite; a program needn't handle non-finite values.
Results may differ from a plain program's by a relative error of at most 0.015.
Values may be sent and summed in bfloat16 or wider, within the bound.
A program may use at most 128 MiB of HBM per device.

v0:
```python
import jax
import jax.numpy as jnp
from jax import lax
from jax.sharding import PartitionSpec as P

NS_ITERS = 3


stat_beta = 0.9
moment_decay = 0.9
square_decay = 0.95
learn_rate = 0.1
epsilon = 1e-08
norm_epsilon = 1e-06
schulz_linear = 3.4445
schulz_cubic = -4.775
schulz_quintic = 2.0315


def schulz_whole(matrix):
    current = matrix
    for sweep_index in range(NS_ITERS):
        gram_matrix = lax.optimization_barrier(
            jnp.dot(current, current.T, preferred_element_type=jnp.float32).astype(jnp.bfloat16)
        )
        poly_matrix = (
            schulz_cubic * gram_matrix.astype(jnp.float32)
            + schulz_quintic * jnp.dot(gram_matrix, gram_matrix, preferred_element_type=jnp.float32)
        ).astype(jnp.bfloat16)
        current = (
            schulz_linear * current.astype(jnp.float32)
            + jnp.dot(poly_matrix, current, preferred_element_type=jnp.float32)
        ).astype(jnp.bfloat16)
    return current


def schulz_split(start_rows):
    current = start_rows
    for sweep_index in range(NS_ITERS):
        gathered = lax.all_gather(current, "shard", axis=1, tiled=True)
        gram_rows = lax.optimization_barrier(
            jnp.einsum(
                "bik,bjk->bij", current, gathered, preferred_element_type=jnp.float32
            ).astype(jnp.bfloat16)
        )
        gram_block = lax.all_gather(gram_rows, "shard", axis=1, tiled=True)
        poly_rows = (
            schulz_cubic * gram_rows.astype(jnp.float32)
            + schulz_quintic
            * jnp.einsum("bij,bjk->bik", gram_rows, gram_block, preferred_element_type=jnp.float32)
        ).astype(jnp.bfloat16)
        current = (
            schulz_linear * current.astype(jnp.float32)
            + jnp.einsum("bij,bjk->bik", poly_rows, gathered, preferred_element_type=jnp.float32)
        ).astype(jnp.bfloat16)
    return current


def on_device(
    grad_parts, weights, stat_left, stat_right, basis_left, basis_right, moment_first, moment_second
):
    block_count = weights.shape[0]
    row_count = weights.shape[1]
    width_kv = weights.shape[2]
    rep_count = lax.axis_size("rep")
    shard_pos = lax.axis_index("shard")
    row_start = shard_pos * row_count
    partial_value = grad_parts[0, 0]
    grad_total = lax.psum(partial_value, ("rep", "shard")) / rep_count
    grad_full = grad_total.astype(jnp.bfloat16)
    grad_rows = lax.dynamic_slice_in_dim(grad_full, row_start, row_count, 1)
    left_new = stat_beta * stat_left + (1.0 - stat_beta) * jnp.einsum(
        "bik,bjk->bij", grad_rows, grad_full, preferred_element_type=jnp.float32
    )
    grad_flat = grad_rows.reshape(block_count * row_count, width_kv)
    right_terms = jnp.dot(grad_flat.T, grad_flat, preferred_element_type=jnp.float32)
    right_new = stat_beta * stat_right + (1.0 - stat_beta) * lax.psum(right_terms, "shard")
    basis_all = lax.all_gather(basis_left, "shard", axis=1, tiled=True)
    power_rows = jnp.einsum(
        "bij,bjk->bik", left_new.astype(jnp.bfloat16), basis_all, preferred_element_type=jnp.float32
    )
    local_squares = jnp.sum(power_rows * power_rows, axis=(1, 2))
    block_squares = lax.psum(local_squares, "shard")
    start_rows = (power_rows * lax.rsqrt(block_squares + norm_epsilon)[:, None, None]).astype(
        jnp.bfloat16
    )
    basis_left_new = schulz_split(start_rows)
    right_power = jnp.dot(
        right_new.astype(jnp.bfloat16), basis_right, preferred_element_type=jnp.float32
    )
    right_start = (
        right_power * lax.rsqrt(jnp.sum(right_power * right_power) + norm_epsilon)
    ).astype(jnp.bfloat16)
    basis_right_new = schulz_whole(right_start)
    local_turn = jnp.einsum(
        "bji,bjk->bik", basis_left, grad_rows, preferred_element_type=jnp.float32
    )
    rot_left = lax.psum_scatter(
        local_turn.astype(jnp.bfloat16), "shard", scatter_dimension=1, tiled=True
    ).astype(jnp.float32)
    rot_flat = rot_left.reshape(block_count * row_count, width_kv).astype(jnp.bfloat16)
    rotated = jnp.dot(rot_flat, basis_right, preferred_element_type=jnp.float32).reshape(
        block_count, row_count, width_kv
    )
    moment_new = moment_decay * moment_first + (1.0 - moment_decay) * rotated
    square_new = square_decay * moment_second + (1.0 - square_decay) * rotated * rotated
    direction = moment_new / (jnp.sqrt(square_new) + epsilon)
    direction_flat = direction.reshape(block_count * row_count, width_kv).astype(jnp.bfloat16)
    half_turn = (
        jnp.dot(direction_flat, basis_right.T, preferred_element_type=jnp.float32)
        .astype(jnp.bfloat16)
        .reshape(block_count, row_count, width_kv)
    )
    half_all = lax.all_gather(half_turn, "shard", axis=1, tiled=True)
    update = jnp.einsum("bij,bjk->bik", basis_left, half_all, preferred_element_type=jnp.float32)
    weight_rows_new = (weights.astype(jnp.float32) - learn_rate * update).astype(jnp.bfloat16)
    weights_new = lax.all_gather(weight_rows_new, "shard", axis=1, tiled=True)
    return (weights_new, basis_left_new, basis_right_new, moment_new, square_new)


def solution(mesh):
    placed = (
        P("rep", "shard", None, None, None),
        P(None, "shard", None),
        P(None, "shard", None),
        P(),
        P(None, "shard", None),
        P(),
        P(None, "shard", None),
        P(None, "shard", None),
    )
    return jax.shard_map(
        on_device,
        mesh=mesh,
        in_specs=placed,
        out_specs=(
            P(),
            P(None, "shard", None),
            P(),
            P(None, "shard", None),
            P(None, "shard", None),
        ),
        check_vma=False,
    )
```

profile of v0, /device:TPU:0, one launch (start us, length us, event | category | flops | bytes accessed | tf_op | source)
XLA Modules:
  0.0 368.9 jit_solution(12095255493840172626)
XLA Ops:
  9.4 149.6 %all-reduce.3.cloned.1.call-done = f32[2,1024,512]{2,1,0:T(8,128)} async-done(((f32[2,1024,512]{2,1,0:T(8,128)}), f32[2,1024,512]{2,1,0:T(8,128)}) %all-reduce.3.cloned.1.call-update) | async-done | bytes 4194320 | tf_op jit(solution)/shard_map/psum | solution.py:69
  158.9 2.8 multiply_convert_fusion.1
  161.8 9.8 %multiply_reduce_fusion = (f32[2]{0:T(128)S(1)}, f32[2,512,1024]{2,1,0:T(8,128)}) fusion(bf16[2,1024,1024]{2,1,0:T(8,128)(2,1)} %all-gather.14.cloned.1.call-done, f32[2,512,1024]{2,1,0:T(8,128)} %param.10, bf16[2,1024,512]{2,1,0:T(8,128)(2,1)S(1)} %multiply_convert_fusion.1, s32[]{:T(128)S(6)} %select_n.3), kind=kOutput, calls=%fused_computation.7 | convolution fusion | flops 3227516928 | bytes 15728652 | tf_op jit(solution)/shard_map/bij,bjk->bik/dot_general | solution.py:79
  174.0 4.1 %multiply_convert_fusion = bf16[2,512,1024]{2,1,0:T(8,128)(2,1)} fusion(f32[2,512,1024]{2,1,0:T(8,128)} %get-tuple-element.14, f32[2]{0:T(128)S(1)} %add_rsqrt_fusion), kind=kLoop, calls=%fused_computation.6 | loop fusion | flops 2097152 | bytes 6291464 | tf_op jit(solution)/shard_map/convert_element_type | solution.py:84
  178.3 12.5 %all-gather.16.cloned.1.call-done = bf16[2,1024,1024]{2,1,0:T(8,128)(2,1)} async-done(((bf16[2,512,1024]{2,1,0:T(8,128)(2,1)}), bf16[2,1024,1024]{2,1,0:T(8,128)(2,1)}) %all-gather.16.cloned.1.call-update) | async-done | bytes 4194320 | tf_op jit(solution)/shard_map/all_gather | solution.py:40
  190.8 6.5 %convolution_convert_fusion.2 = bf16[2,512,1024]{2,1,0:T(8,128)(2,1)} fusion(bf16[2,512,1024]{2,1,0:T(8,128)(2,1)} %multiply_convert_fusion, bf16[2,1024,1024]{2,1,0:T(8,128)(2,1)} %all-gather.16.cloned.1.call-done), kind=kOutput, calls=%fused_computation.19 | convolution fusion | flops 2148532224 | bytes 8388608 | tf_op jit(solution)/shard_map/bik,bjk->bij/dot_general | solution.py:42
  197.4 14.8 %all-gather.18.cloned.1.call-done = bf16[2,1024,1024]{2,1,0:T(8,128)(2,1)} async-done(((bf16[2,512,1024]{2,1,0:T(8,128)(2,1)}), bf16[2,1024,1024]{2,1,0:T(8,128)(2,1)}) %all-gather.18.cloned.1.call-update) | async-done | bytes 4194320 | tf_op jit(solution)/shard_map/all_gather | solution.py:46
  212.2 10.7 %add_convert_fusion.4 = bf16[2,512,1024]{2,1,0:T(8,128)(2,1)} fusion(bf16[2,512,1024]{2,1,0:T(8,128)(2,1)S(1)} %copy-done.1, bf16[2,1024,1024]{2,1,0:T(8,128)(2,1)} %all-gather.16.cloned.1.call-done, bf16[2,512,1024]{2,1,0:T(8,128)(2,1)} %convolution_convert_fusion.2, bf16[2,1024,1024]{2,1,0:T(8,128)(2,1)} %all-gather.18.cloned.1.call-done), kind=kOutput, calls=%fused_computation.4 | convolution fusion | flops 4304404480 | bytes 14680064 | tf_op jit(solution)/shard_map/bij,bjk->bik/dot_general | solution.py:54
  223.0 4.7 %convert_bitcast_fusion = bf16[2,1024,512]{2,1,0:T(8,128)(2,1)} fusion(bf16[2,512,1024]{2,1,0:T(8,128)(2,1)} %param.12, bf16[2,1024,512]{2,1,0:T(8,128)(2,1)} %copy-done.2, s32[]{:T(128)S(6)} %select_n.3), kind=kOutput, calls=%fused_computation.16 | convolution fusion | flops 1074790400 | bytes 5242884 | tf_op jit(solution)/shard_map/bji,bjk->bik/dot_general | solution.py:95
  227.9 9.9 %all-gather.20.cloned.1.call-done = bf16[2,1024,1024]{2,1,0:T(8,128)(2,1)} async-done(((bf16[2,512,1024]{2,1,0:T(8,128)(2,1)}), bf16[2,1024,1024]{2,1,0:T(8,128)(2,1)}) %all-gather.20.cloned.1.call-update) | async-done | bytes 4194320 | tf_op jit(solution)/shard_map/all_gather | solution.py:40
  237.8 5.9 %convolution_convert_fusion.1 = bf16[2,512,1024]{2,1,0:T(8,128)(2,1)} fusion(bf16[2,512,1024]{2,1,0:T(8,128)(2,1)S(1)} %copy-done.6, bf16[2,1024,1024]{2,1,0:T(8,128)(2,1)} %all-gather.20.cloned.1.call-done), kind=kOutput, calls=%fused_computation.18 | convolution fusion | flops 2148532224 | bytes 8388608 | tf_op jit(solution)/shard_map/bik,bjk->bij/dot_general | solution.py:42
  243.7 7.7 %reduce-scatter.2.cloned.1.call-done = bf16[2,512,512]{2,1,0:T(8,128)(2,1)} async-done(((bf16[2,1024,512]{2,1,0:T(8,128)(2,1)}), bf16[2,512,512]{2,1,0:T(8,128)(2,1)}) %reduce-scatter.2.cloned.1.call-update) | async-done | bytes 1048592 | tf_op jit(solution)/shard_map/reduce_scatter | solution.py:98
  251.4 6.2 %divide_convert_fusion = (bf16[2,512,512]{2,1,0:T(8,128)(2,1)S(1)}, f32[2,512,512]{2,1,0:T(8,128)}, f32[2,512,512]{2,1,0:T(8,128)}) fusion(f32[2,512,512]{2,1,0:T(8,128)} %param.15, f32[2,512,512]{2,1,0:T(8,128)} %param.14, bf16[2,512,512]{2,1,0:T(8,128)(2,1)} %reduce-scatter.2.cloned.1.call-done, bf16[512,512]{1,0:T(8,128)(2,1)S(1)} %copy-done), kind=kOutput, calls=%fused_computation.14 | convolution fusion | flops 542113792 | bytes 11010048 | tf_op jit(solution)/shard_map/dot_general | solution.py:102
  259.7 8.1 %all-gather.22.cloned.1.call-done = bf16[2,1024,1024]{2,1,0:T(8,128)(2,1)} async-done(((bf16[2,512,1024]{2,1,0:T(8,128)(2,1)}), bf16[2,1024,1024]{2,1,0:T(8,128)(2,1)}) %all-gather.22.cloned.1.call-update) | async-done | bytes 4194320 | tf_op jit(solution)/shard_map/all_gather | solution.py:46
  267.8 11.3 %add_convert_fusion.2 = bf16[2,512,1024]{2,1,0:T(8,128)(2,1)} fusion(bf16[2,512,1024]{2,1,0:T(8,128)(2,1)} %add_convert_fusion.4, bf16[2,1024,1024]{2,1,0:T(8,128)(2,1)} %all-gather.20.cloned.1.call-done, bf16[2,512,1024]{2,1,0:T(8,128)(2,1)} %convolution_convert_fusion.1, bf16[2,1024,1024]{2,1,0:T(8,128)(2,1)} %all-gather.22.cloned.1.call-done), kind=kOutput, calls=%fused_computation.2 | convolution fusion | flops 4304404480 | bytes 14680064 | tf_op jit(solution)/shard_map/bij,bjk->bik/dot_general | solution.py:54
  283.3 4.9 %fusion.1 = bf16[2,512,512]{1,2,0:T(8,128)(2,1)} fusion(bf16[2,512,512]{1,2,0:T(8,128)(2,1)} %copy.13, bf16[2,1024,512]{1,2,0:T(8,128)(2,1)} %all-gather.10.cloned.1.call-done, bf16[2,512,1024]{2,1,0:T(8,128)(2,1)} %param.12), kind=kOutput, calls=%fused_computation.13 | convolution fusion | flops 1075838976 | bytes 6291456 | tf_op jit(solution)/shard_map/bij,bjk->bik/dot_general | solution.py:115
  288.4 9.4 %all-gather.24.cloned.1.call-done = bf16[2,1024,1024]{2,1,0:T(8,128)(2,1)} async-done(((bf16[2,512,1024]{2,1,0:T(8,128)(2,1)}), bf16[2,1024,1024]{2,1,0:T(8,128)(2,1)}) %all-gather.24.cloned.1.call-update) | async-done | bytes 4194320 | tf_op jit(solution)/shard_map/all_gather | solution.py:40
  297.8 5.9 %convolution_convert_fusion = bf16[2,512,1024]{2,1,0:T(8,128)(2,1)} fusion(bf16[2,512,1024]{2,1,0:T(8,128)(2,1)S(1)} %copy-done.4, bf16[2,1024,1024]{2,1,0:T(8,128)(2,1)} %all-gather.24.cloned.1.call-done), kind=kOutput, calls=%fused_computation.17 | convolution fusion | flops 2148532224 | bytes 8388608 | tf_op jit(solution)/shard_map/bik,bjk->bij/dot_general | solution.py:42
  303.8 16.8 %all-reduce.5.cloned.1.call-done = f32[512,512]{1,0:T(8,128)} async-done(((f32[512,512]{1,0:T(8,128)}), f32[512,512]{1,0:T(8,128)}) %all-reduce.5.cloned.1.call-update) | async-done | bytes 1048592 | tf_op jit(solution)/shard_map/psum | solution.py:77
  327.7 3.1 fusion.10
  330.8 3.6 all-gather.12.cloned.1.call-done
  334.4 3.9 %copy.15 = bf16[2,1024,512]{2,1,0:T(8,128)(2,1)} copy(bf16[2,1024,512]{1,2,0:T(8,128)(2,1)} %all-gather.12.cloned.1.call-done) | data formatting | bytes 4194304
  338.4 12.3 %all-gather.26.cloned.1.call-done = bf16[2,1024,1024]{2,1,0:T(8,128)(2,1)} async-done(((bf16[2,512,1024]{2,1,0:T(8,128)(2,1)}), bf16[2,1024,1024]{2,1,0:T(8,128)(2,1)}) %all-gather.26.cloned.1.call-update) | async-done | bytes 4194320 | tf_op jit(solution)/shard_map/all_gather | solution.py:46
  350.6 10.7 %add_convert_fusion = bf16[2,512,1024]{2,1,0:T(8,128)(2,1)} fusion(bf16[2,512,1024]{2,1,0:T(8,128)(2,1)S(1)} %copy-done.5, bf16[2,1024,1024]{2,1,0:T(8,128)(2,1)} %all-gather.24.cloned.1.call-done, bf16[2,512,1024]{2,1,0:T(8,128)(2,1)} %convolution_convert_fusion, bf16[2,1024,1024]{2,1,0:T(8,128)(2,1)} %all-gather.26.cloned.1.call-done), kind=kOutput, calls=%fused_computation | convolution fusion | flops 4304404480 | bytes 14680064 | tf_op jit(solution)/shard_map/bij,bjk->bik/dot_general | solution.py:54
  (52 shorter events, 17.3 us)
Async XLA Ops:
  8.0 243.4 %copy-start = (bf16[512,512]{1,0:T(8,128)(2,1)S(1)}, bf16[512,512]{1,0:T(8,128)(2,1)}, u32[]{:S(2)}) copy-start(bf16[512,512]{1,0:T(8,128)(2,1)} %param.13) | copy-start | bytes 1572868
  8.0 150.9 %all-reduce.3.cloned.1.call-start = ((), (), s32[]{:S(2)}) async-start(), calls=%async_computation.1 | async-start | bytes 8388608 | tf_op jit(solution)/shard_map/psum | solution.py:69
  8.7 153.0 %all-gather.14.cloned.1.call-start = ((), (), s32[]{:S(2)}) async-start(), calls=%async_computation.5 | async-start | bytes 6291456 | tf_op jit(solution)/shard_map/all_gather | solution.py:78
  9.3 181.4 %all-gather.16.cloned.1.call-start = ((), (), s32[]{:S(2)}) async-start(), calls=%async_computation.6 | async-start | bytes 6291456 | tf_op jit(solution)/shard_map/all_gather | solution.py:40
  161.7 9.9 %copy-start.2 = (bf16[2,1024,512]{2,1,0:T(8,128)(2,1)}, bf16[2,1024,512]{2,1,0:T(8,128)(2,1)S(1)}, u32[]{:S(2)}) copy-start(bf16[2,1024,512]{2,1,0:T(8,128)(2,1)S(1)} %multiply_convert_fusion.1) | copy-start | bytes 6291460
  178.2 34.0 %copy-start.1 = (bf16[2,512,1024]{2,1,0:T(8,128)(2,1)S(1)}, bf16[2,512,1024]{2,1,0:T(8,128)(2,1)}, u32[]{:S(2)}) copy-start(bf16[2,512,1024]{2,1,0:T(8,128)(2,1)} %multiply_convert_fusion) | copy-start | bytes 6291460
  178.2 33.9 %all-gather.18.cloned.1.call-start = ((), (), s32[]{:S(2)}) async-start(), calls=%async_computation.7 | async-start | bytes 6291456 | tf_op jit(solution)/shard_map/all_gather | solution.py:46
  197.3 40.5 %all-gather.20.cloned.1.call-start = ((), (), s32[]{:S(2)}) async-start(), calls=%async_computation.8 | async-start | bytes 6291456 | tf_op jit(solution)/shard_map/all_gather | solution.py:40
  222.9 14.9 %copy-start.6 = (bf16[2,512,1024]{2,1,0:T(8,128)(2,1)S(1)}, bf16[2,512,1024]{2,1,0:T(8,128)(2,1)}, u32[]{:S(2)}) copy-start(bf16[2,512,1024]{2,1,0:T(8,128)(2,1)} %add_convert_fusion.4) | copy-start | bytes 6291460
  222.9 28.5 %reduce-scatter.2.cloned.1.call-start = ((), (), s32[]{:S(2)}) async-start(), calls=%async_computation.2 | async-start | bytes 3145728 | tf_op jit(solution)/shard_map/reduce_scatter | solution.py:98
  227.7 40.1 %all-gather.22.cloned.1.call-start = ((), (), s32[]{:S(2)}) async-start(), calls=%async_computation.9 | async-start | bytes 6291456 | tf_op jit(solution)/shard_map/all_gather | solution.py:46
  243.7 39.6 %all-gather.10.cloned.1.call-start = ((), (), s32[]{:S(2)}) async-start(), calls=%async_computation.3 | async-start | bytes 3145728 | tf_op jit(solution)/shard_map/all_gather | solution.py:114
  259.6 19.5 %copy-start.3 = (bf16[2,1024,512]{2,1,0:T(8,128)(2,1)S(1)}, bf16[2,1024,512]{2,1,0:T(8,128)(2,1)}, u32[]{:S(2)}) copy-start(bf16[2,1024,512]{2,1,0:T(8,128)(2,1)} %copy-done.2) | copy-start | bytes 6291460
  259.6 38.2 %all-gather.24.cloned.1.call-start = ((), (), s32[]{:S(2)}) async-start(), calls=%async_computation.10 | async-start | bytes 6291456 | tf_op jit(solution)/shard_map/all_gather | solution.py:40
  279.1 41.5 %all-reduce.5.cloned.1.call-start = ((), (), s32[]{:S(2)}) async-start(), calls=%async_computation.12 | async-start | bytes 2097152 | tf_op jit(solution)/shard_map/psum | solution.py:77
  280.9 53.5 %all-gather.12.cloned.1.call-start = ((), (), s32[]{:S(2)}) async-start(), calls=%async_computation.4 | async-start | bytes 3145728 | tf_op jit(solution)/shard_map/all_gather | solution.py:117
  283.2 14.6 %copy-start.4 = (bf16[2,512,1024]{2,1,0:T(8,128)(2,1)S(1)}, bf16[2,512,1024]{2,1,0:T(8,128)(2,1)}, u32[]{:S(2)}) copy-start(bf16[2,512,1024]{2,1,0:T(8,128)(2,1)} %add_convert_fusion.2) | copy-start | bytes 6291460
  288.2 62.5 %all-gather.26.cloned.1.call-start = ((), (), s32[]{:S(2)}) async-start(), calls=%async_computation.11 | async-start | bytes 6291456 | tf_op jit(solution)/shard_map/all_gather | solution.py:46
  327.7 22.9 %copy-start.5 = (bf16[2,512,1024]{2,1,0:T(8,128)(2,1)S(1)}, bf16[2,512,1024]{2,1,0:T(8,128)(2,1)}, u32[]{:S(2)}) copy-start(bf16[2,512,1024]{2,1,0:T(8,128)(2,1)} %add_convert_fusion.2) | copy-start | bytes 6291460
Sparse Core Ops, SparseCore 0:
  14.4 144.5 all-reduce.2
Sparse Core Ops, SparseCore 1:
  10.8 16.3 all-gather.13
  178.3 12.4 all-gather.15
  197.4 14.7 all-gather.17
  223.0 14.7 all-gather.19
  240.6 10.7 reduce-scatter.1
  253.0 14.7 all-gather.21
  269.8 11.6 all-gather.9
  283.0 14.7 all-gather.23
  300.1 20.4 all-reduce.4
  322.7 11.6 all-gather.11
  335.9 14.7 all-gather.25
where the time goes:
time: 369 us
  waiting for transfers between devices  246 us (67%)
  matrix products  88.6 us (24%)
  between operations  16.6 us (4%)
  local copies, waits for them, and re-layouts  7.58 us (2%)
  other arithmetic  6.91 us (2%)
    psum x1, waiting for transfers between devices, on_device(): grad_total = lax.psum(partial_value, ('rep', 'shard')) / rep_count  150 us
    all_gather x3, waiting for transfers between devices, schulz_split(): gram_block = lax.all_gather(gram_rows, 'shard', axis=1, tiled=True)  35.2 us
    dot_general x3, matrix products, schulz_split(): jnp.einsum('bij,bjk->bik', poly_rows, gathered, preferred_element_type=jn...  32.7 us
    all_gather x3, waiting for transfers between devices, schulz_split(): gathered = lax.all_gather(current, 'shard', axis=1, tiled=True)  31.7 us
    dot_general x3, matrix products, schulz_split(): jnp.einsum('bik,bjk->bij', current, gathered, preferred_element_type=jnp....  18.3 us
    psum x1, waiting for transfers between devices, on_device(): lax.psum(right_terms, 'shard')  16.8 us
    dot_general x1, matrix products, on_device(): jnp.einsum('bij,bjk->bik', left_new.astype(jnp.bfloat16), basis_all, pref...  9.84 us
    reduce_scatter x1, waiting for transfers between devices, on_device(): lax.psum_scatter(local_turn.astype(jnp.bfloat16), 'shard', scatter_dimens...  7.67 us
  transfers between devices with their start and end apart: 12, of which 10 were waited for; matrix products, arithmetic and copies ran while one was open for 17% of the time, Pallas kernels for 0%

commit v1 on v0

--- a/solution.py
+++ b/solution.py
@@ -1,6 +1,10 @@
+import functools
+
 import jax
 import jax.numpy as jnp
 from jax import lax
+from jax.experimental import pallas as pl
+from jax.experimental.pallas import tpu as pltpu
 from jax.sharding import PartitionSpec as P
 
 NS_ITERS = 3
@@ -118,7 +122,340 @@
     return (weights_new, basis_left_new, basis_right_new, moment_new, square_new)
 
 
+MESH = pl.DeviceIdType.MESH
+PLANE = 4
+LINE = 4
+ORDER = (2, 1, 3, 0)
+F32 = jnp.float32
+BF16 = jnp.bfloat16
+
+
+def gather_kernel(
+    parts, basis, stat, first, second, weights,
+    grad_out, basis_out, stat_out, first_out, second_out, weights_out,
+    far_part, near_part, pair_send, pair_recv, chip_low, plane_recv, line_send, line_recv,
+    load_sem, pair_sem, plane_sem, line_sem, gline_sem, gplane_sem, gpair_sem, swap_sem, keep_sem,
+):
+    rep = lax.axis_index("rep")
+    core = lax.axis_index("shard")
+    other = 1 - core
+    layer = rep // PLANE
+    spot = lax.rem(rep, PLANE)
+    height = basis.shape[1]
+
+    def line_of(k):
+        return lax.rem(layer + k, LINE)
+
+    def spot_of(j):
+        return lax.rem(spot + j, PLANE)
+
+    loads = {}
+    for k in ORDER:
+        far = pltpu.make_async_copy(parts.at[other, :, line_of(k)], far_part.at[k], load_sem.at[0, k])
+        near = pltpu.make_async_copy(parts.at[core, :, line_of(k)], near_part.at[k], load_sem.at[1, k])
+        far.start()
+        near.start()
+        loads[k] = (far, near)
+
+    barrier = pltpu.get_barrier_semaphore()
+    partners = [(rep, other)]
+    partners += [(layer * PLANE + spot_of(j), core) for j in range(1, PLANE)]
+    partners += [(line_of(k) * PLANE + spot, core) for k in range(1, LINE)]
+    for partner in partners:
+        pl.semaphore_signal(barrier, inc=1, device_id=partner, device_id_type=MESH)
+    pl.semaphore_wait(barrier, len(partners))
+
+    def send(source, target, sems, partner):
+        copy = pltpu.make_async_remote_copy(
+            src_ref=source, dst_ref=target, send_sem=sems.at[0], recv_sem=sems.at[1],
+            device_id=partner, device_id_type=MESH,
+        )
+        copy.start()
+        return copy
+
+    sent = []
+    pairs = {}
+    for k in ORDER:
+        loads[k][0].wait()
+        pair_send[k] = far_part[k].astype(BF16)
+        pairs[k] = send(pair_send.at[k], pair_recv.at[k], pair_sem.at[k], (rep, other))
+
+    planes = {}
+    for k in ORDER:
+        loads[k][1].wait()
+        pairs[k].wait_recv()
+        near_part[k] = near_part[k] + pair_recv[k].astype(F32)
+        chip_low[k] = near_part[k].astype(BF16)
+        for j in (2, 1, 3):
+            planes[k, j] = send(
+                chip_low.at[k, spot_of(j)], plane_recv.at[k, j - 1], plane_sem.at[k, j - 1],
+                (layer * PLANE + spot_of(j), core),
+            )
+
+    mine = pl.ds(pl.multiple_of(core * height, height), height)
+    swaps = []
+    keeps = []
+    moved = ((basis, basis_out), (stat, stat_out), (first, first_out), (second, second_out), (weights, weights_out))
+    for at, (source, target) in enumerate(moved):
+        swaps.append(send(source.at[other], target.at[mine], swap_sem.at[at], (rep, other)))
+        keep = pltpu.make_async_copy(source.at[core], target.at[mine], keep_sem.at[at])
+        keep.start()
+        keeps.append(keep)
+
+    lines = {}
+    total = None
+    for k in ORDER:
+        for j in range(1, PLANE):
+            planes[k, j].wait_recv()
+        total = near_part[k, spot]
+        for j in range(1, PLANE):
+            total = total + plane_recv[k, j - 1].astype(F32)
+        if k:
+            line_send[k - 1] = total.astype(BF16)
+            lines[k] = send(
+                line_send.at[k - 1], line_recv.at[k - 1], line_sem.at[k - 1],
+                (line_of(k) * PLANE + spot, core),
+            )
+    for k in range(1, LINE):
+        lines[k].wait_recv()
+        total = total + line_recv[k - 1].astype(F32)
+    grad_out[core, spot, layer] = (total * (1.0 / (PLANE * LINE))).astype(BF16)
+
+    def share(piece, sems, partner):
+        return send(grad_out.at[piece], grad_out.at[piece], sems, partner)
+
+    own = (core, spot, layer)
+    glines = {k: share(own, gline_sem.at[k - 1], (line_of(k) * PLANE + spot, core)) for k in (2, 1, 3)}
+    gplanes = {}
+    gpairs = []
+    for k in (0, 1, 3, 2):
+        piece = (core, spot, lax.rem(layer + LINE - k, LINE))
+        if k:
+            glines[k].wait_recv()
+        for j in (2, 1, 3):
+            gplanes[k, j] = share(piece, gplane_sem.at[k, j - 1], (layer * PLANE + spot_of(j), core))
+        gpairs.append(share(piece, gpair_sem.at[k, 0], (rep, other)))
+    for k in (0, 1, 3, 2):
+        for j in (1, 3, 2):
+            gplanes[k, j].wait_recv()
+            piece = (core, lax.rem(spot + PLANE - j, PLANE), lax.rem(layer + LINE - k, LINE))
+            gpairs.append(share(piece, gpair_sem.at[k, j], (rep, other)))
+    for copy in gpairs + swaps:
+        copy.wait_recv()
+    for group in (pairs, planes, lines, glines, gplanes):
+        sent += list(group.values())
+    for copy in sent + gpairs + swaps:
+        copy.wait_send()
+    for keep in keeps:
+        keep.wait()
+
+
+def gather_inputs(grad_parts, basis, stat, first, second, weights):
+    blocks, height, width = weights.shape
+    block = 2 * height
+    piece = block // (PLANE * LINE)
+    parts = grad_parts.reshape(blocks, PLANE, LINE, piece, width)
+    anywhere = pl.BlockSpec(memory_space=pl.ANY)
+    dma = pltpu.SemaphoreType.DMA
+    out = pl.pallas_call(
+        gather_kernel,
+        out_shape=(
+            jax.ShapeDtypeStruct((blocks, PLANE, LINE, piece, width), BF16),
+            jax.ShapeDtypeStruct((block, block), BF16),
+            jax.ShapeDtypeStruct((block, block), F32),
+            jax.ShapeDtypeStruct((block, width), F32),
+            jax.ShapeDtypeStruct((block, width), F32),
+            jax.ShapeDtypeStruct((block, width), BF16),
+        ),
+        in_specs=[anywhere] * 6,
+        out_specs=(pl.BlockSpec(memory_space=pltpu.VMEM),) + (anywhere,) * 5,
+        scratch_shapes=[
+            pltpu.VMEM((LINE, PLANE, piece, width), F32),
+            pltpu.VMEM((LINE, PLANE, piece, width), F32),
+            pltpu.VMEM((LINE, PLANE, piece, width), BF16),
+            pltpu.VMEM((LINE, PLANE, piece, width), BF16),
+            pltpu.VMEM((LINE, PLANE, piece, width), BF16),
+            pltpu.VMEM((LINE, PLANE - 1, piece, width), BF16),
+            pltpu.VMEM((LINE - 1, piece, width), BF16),
+            pltpu.VMEM((LINE - 1, piece, width), BF16),
+            dma((2, LINE)),
+            dma((LINE, 2)),
+            dma((LINE, PLANE - 1, 2)),
+            dma((LINE - 1, 2)),
+            dma((LINE - 1, 2)),
+            dma((LINE, PLANE - 1, 2)),
+            dma((LINE, PLANE, 2)),
+            dma((5, 2)),
+            dma((5,)),
+        ],
+        compiler_params=pltpu.CompilerParams(
+            collective_id=0, has_side_effects=True, vmem_limit_bytes=40 << 20
+        ),
+    )(parts, basis, stat, first, second, weights)
+    return (out[0].reshape(blocks, block, width),) + tuple(out[1:])
+
+
+def dot(a, b, dims=((1,), (0,))):
+    return lax.dot_general(a, b, (dims, ((), ())), preferred_element_type=F32)
+
+
+def turn_kernel(grad, basis, right, first, second, weights, first_out, second_out, weights_out, half):
+    core = lax.axis_index("shard")
+    tile = 256
+
+    @pl.loop(0, basis.shape[0] // tile)
+    def _(at):
+        rows = pl.ds(pl.multiple_of(at * tile, tile), tile)
+        rot = dot(basis[:, rows], grad[core], ((0,), (0,)))
+        rotated = dot(rot.astype(BF16), right[...])
+        moment = moment_decay * first[rows, :] + (1.0 - moment_decay) * rotated
+        square = square_decay * second[rows, :] + (1.0 - square_decay) * rotated * rotated
+        first_out[rows, :] = moment
+        second_out[rows, :] = square
+        direction = moment / (jnp.sqrt(square) + epsilon)
+        half[rows, :] = dot(direction.astype(BF16), right[...], ((1,), (1,))).astype(BF16)
+
+    @pl.loop(0, basis.shape[0] // tile)
+    def _(at):
+        rows = pl.ds(pl.multiple_of(at * tile, tile), tile)
+        update = dot(basis[rows, :], half[...])
+        weights_out[rows, :] = (weights[rows, :].astype(F32) - learn_rate * update).astype(BF16)
+
+
+def turn_block(grad, basis, right, first, second, weights):
+    in_vmem = pl.BlockSpec(memory_space=pltpu.VMEM)
+    return pl.pallas_call(
+        turn_kernel,
+        out_shape=(
+            jax.ShapeDtypeStruct(first.shape, F32),
+            jax.ShapeDtypeStruct(second.shape, F32),
+            jax.ShapeDtypeStruct(weights.shape, BF16),
+        ),
+        in_specs=[in_vmem] * 6,
+        out_specs=(in_vmem,) * 3,
+        scratch_shapes=[pltpu.VMEM(weights.shape, BF16)],
+        compiler_params=pltpu.CompilerParams(vmem_limit_bytes=40 << 20),
+        cost_estimate=pl.CostEstimate(flops=3 << 30, bytes_accessed=16 << 20, transcendentals=0),
+    )(grad, basis, right, first, second, weights)
+
+
+def schulz_sweeps(start, gram, spare, out, size, tile):
+    tiles = size // tile
+    chain = [start, spare, start, out]
+    for sweep in range(NS_ITERS):
+        now, later = chain[sweep], (out if sweep == NS_ITERS - 1 else chain[sweep + 1])
+
+        @pl.loop(0, tiles)
+        def _(at):
+            rows = pl.ds(pl.multiple_of(at * tile, tile), tile)
+            gram[rows, :] = dot(now[rows, :], now[...], ((1,), (1,))).astype(BF16)
+
+        @pl.loop(0, tiles)
+        def _(at):
+            rows = pl.ds(pl.multiple_of(at * tile, tile), tile)
+            poly = schulz_cubic * gram[rows, :].astype(F32) + schulz_quintic * dot(gram[rows, :], gram[...])
+            later[rows, :] = (
+                schulz_linear * now[rows, :].astype(F32) + dot(poly.astype(BF16), now[...])
+            ).astype(BF16)
+
+
+def basis_kernel(
+    grad, stat, basis, stat_right, right, left_out, right_out,
+    power, start, spare, gram, rpower, rstart, rspare, rgram,
+):
+    core = lax.axis_index("shard")
+    size = basis.shape[0]
+    width = right.shape[0]
+    tile = 256
+
+    def left_tile(at, total):
+        rows = pl.ds(pl.multiple_of(at * tile, tile), tile)
+        mixed = stat_beta * stat[rows, :] + (1.0 - stat_beta) * dot(
+            grad[core, rows, :], grad[core], ((1,), (1,))
+        )
+        value = dot(mixed.astype(BF16), basis[...])
+        power[rows, :] = value
+        return total + jnp.sum(value * value)
+
+    total = lax.fori_loop(0, size // tile, left_tile, jnp.float32(0.0))
+    scale = lax.rsqrt(total + norm_epsilon)
+
+    @pl.loop(0, size // tile)
+    def _(at):
+        rows = pl.ds(pl.multiple_of(at * tile, tile), tile)
+        start[rows, :] = (power[rows, :] * scale).astype(BF16)
+
+    schulz_sweeps(start, gram, spare, left_out, size, tile)
+
+    def right_tile(at, total):
+        rows = pl.ds(pl.multiple_of(at * tile, tile), tile)
+        terms = dot(grad[0, :, rows], grad[0], ((0,), (0,))) + dot(grad[1, :, rows], grad[1], ((0,), (0,)))
+        mixed = stat_beta * stat_right[rows, :] + (1.0 - stat_beta) * terms
+        value = dot(mixed.astype(BF16), right[...])
+        rpower[rows, :] = value
+        return total + jnp.sum(value * value)
+
+    rtotal = lax.fori_loop(0, width // tile, right_tile, jnp.float32(0.0))
+    rscale = lax.rsqrt(rtotal + norm_epsilon)
+    rstart[...] = (rpower[...] * rscale).astype(BF16)
+    schulz_sweeps(rstart, rgram, rspare, right_out, width, tile)
+
+
+def new_bases(grad, stat, basis, stat_right, right):
+    in_vmem = pl.BlockSpec(memory_space=pltpu.VMEM)
+    size, width = basis.shape[0], right.shape[0]
+    return pl.pallas_call(
+        basis_kernel,
+        out_shape=(jax.ShapeDtypeStruct(basis.shape, BF16), jax.ShapeDtypeStruct(right.shape, BF16)),
+        in_specs=[in_vmem] * 5,
+        out_specs=(in_vmem,) * 2,
+        scratch_shapes=[
+            pltpu.VMEM((size, size), F32),
+            pltpu.VMEM((size, size), BF16),
+            pltpu.VMEM((size, size), BF16),
+            pltpu.VMEM((size, size), BF16),
+            pltpu.VMEM((width, width), F32),
+            pltpu.VMEM((width, width), BF16),
+            pltpu.VMEM((width, width), BF16),
+            pltpu.VMEM((width, width), BF16),
+        ],
+        compiler_params=pltpu.CompilerParams(vmem_limit_bytes=48 << 20),
+        cost_estimate=pl.CostEstimate(flops=26 << 30, bytes_accessed=16 << 20, transcendentals=0),
+    )(grad, stat, basis, stat_right, right)
+
+
+def on_device_blocks(
+    grad_parts, weights, stat_left, stat_right, basis_left, basis_right, moment_first, moment_second
+):
+    height = weights.shape[1]
+    core = lax.axis_index("shard")
+    grad, basis, stat, first, second, rows = gather_inputs(
+        grad_parts, basis_left, stat_left, moment_first, moment_second, weights
+    )
+    first_new, second_new, weights_block = turn_block(grad, basis, basis_right, first, second, rows)
+
+    def halves(value):
+        keep = lax.dynamic_slice_in_dim(value, core * height, height, 0)
+        give = lax.dynamic_slice_in_dim(value, (1 - core) * height, height, 0)
+        take = lax.ppermute(give, "shard", ((0, 1), (1, 0)))
+        return join(keep, take)
+
+    def join(keep, take):
+        low = jnp.where(core == 0, keep, take)
+        high = jnp.where(core == 0, take, keep)
+        return jnp.stack((low, high))
+
+    moment_new = halves(first_new)
+    square_new = halves(second_new)
+    weights_new = join(weights_block, lax.ppermute(weights_block, "shard", ((0, 1), (1, 0))))
+    left_block, basis_right_new = new_bases(grad, stat, basis, stat_right, basis_right)
+    basis_left_new = halves(left_block)
+    return (weights_new, basis_left_new, basis_right_new, moment_new, square_new)
+
+
 def solution(mesh):
+    fits = mesh.shape["shard"] == 2 and mesh.shape["rep"] == 16
+    body = on_device_blocks if fits else on_device
     placed = (
         P("rep", "shard", None, None, None),
         P(None, "shard", None),
@@ -130,7 +467,7 @@
         P(None, "shard", None),
     )
     return jax.shard_map(
-        on_device,
+        body,
         mesh=mesh,
         in_specs=placed,
         out_specs=(

time: 369 us -> 147 us (0.40)
  waiting for transfers between devices: 246 us -> 0.01 us
  Pallas kernels: 0 us -> 123 us
  matrix products: 88.6 us -> 0 us
  between operations: 16.6 us -> 0.74 us
  other arithmetic: 6.91 us -> 12.4 us
    psum x2 -> x0, waiting for transfers between devices: 166 us -> none  [the longest x1 150 us: on_device(): grad_total = lax.psum(partial_value, ('rep', 'shard')) / rep_count]
    pallas_call x0 -> x3, Pallas kernels: none -> 123 us  [the longest x1 72.7 us: gather_inputs(): pl.pallas_call(gather_kernel, out_shape=(jax.ShapeDtypeStruct((blocks, PL...]
    dot_general x19 -> x0, matrix products: 88.6 us -> none  [the longest x3 32.7 us: schulz_split(): jnp.einsum('bij,bjk->bik', poly_rows, gathered, preferred_element_type=jn...]
    all_gather x9 -> x0, waiting for transfers between devices: 70.5 us -> none  [the longest x3 35.2 us: schulz_split(): gram_block = lax.all_gather(gram_rows, 'shard', axis=1, tiled=True)]
    another operation x0 -> x8, other arithmetic: none -> 12.4 us  [join(): return jnp.stack((low, high))]
    reduce_scatter x1 -> x0, waiting for transfers between devices: 7.67 us -> none  [on_device(): lax.psum_scatter(local_turn.astype(jnp.bfloat16), 'shard', scatter_dimens...]
    convert_element_type x2 -> x0, other arithmetic: 6.9 us -> none  [the longest x1 4.14 us: on_device(): (power_rows * lax.rsqrt(block_squares + norm_epsilon)[:, None, None]).ast...]
  transfers between devices with their start and end apart: 12 -> 4, of which waited for: 10 -> 0; matrix products, arithmetic and copies ran while one was open for 17% -> 8% of each run, Pallas kernels for 0% -> 28%
where the time goes in v1:
time: 147 us
  Pallas kernels  123 us (84%)
  other arithmetic  12.4 us (8%)
  local copies, waits for them, and re-layouts  9.39 us (6%)
    pallas_call x1, Pallas kernels, gather_inputs(): pl.pallas_call(gather_kernel, out_shape=(jax.ShapeDtypeStruct((blocks, PL...  72.7 us
    pallas_call x1, Pallas kernels, new_bases(): pl.pallas_call(basis_kernel, out_shape=(jax.ShapeDtypeStruct(basis.shape,...  41.5 us
    another operation x8, other arithmetic, join(): return jnp.stack((low, high))  12.4 us
    pallas_call x1, Pallas kernels, turn_block(): pl.pallas_call(turn_kernel, out_shape=(jax.ShapeDtypeStruct(first.shape,...  8.51 us
    unnamed x18, local copies, waits for them, and re-layouts  6.26 us
    dynamic_slice x3, local copies, waits for them, and re-layouts, halves(): give = lax.dynamic_slice_in_dim(value, (1 - core) * height, height, 0)  3.13 us
  transfers between devices with their start and end apart: 4, of which 0 were waited for; matrix products, arithmetic and copies ran while one was open for 8% of the time, Pallas kernels for 28%

profile of v1, /device:TPU:0, one launch (start us, length us, event | category | flops | bytes accessed | tf_op | source)
XLA Modules:
  0.0 146.7 jit_solution(6839094196179286564)
XLA Ops:
  0.6 1.6 %copy-done = bf16[2,512,1024]{2,1,0:T(8,128)(2,1)S(1)} copy-done((bf16[2,512,1024]{2,1,0:T(8,128)(2,1)S(1)}, bf16[2,512,1024]{2,1,0:T(8,128)(2,1)}, u32[]{:S(2)}) %copy-start) | copy-done | bytes 2097176
  2.2 1.2 copy-done.4
  3.5 72.7 %shard_map.119 = (bf16[2,4,4,64,512]{4,3,2,1,0:T(8,128)(2,1)S(1)}, bf16[1024,1024]{1,0:T(8,128)(2,1)S(1)}, f32[1024,1024]{1,0:T(8,128)}, f32[1024,512]{1,0:T(8,1...) custom-call(f32[2,4,4,64,512]{4,3,2,1,0:T(8,128)} %bitcast.20, bf16[2,512,1024]{2,1,0:T(8,128)(2,1)S(1)} %copy-done, ...), custom_call_target="tpu_custom_call" | custom-call | tf_op jit(solution)/shard_map/pallas_call | solution.py:260
  76.2 0.0 copy-start.6
  76.2 1.3 copy-done.6
  77.5 8.5 %shard_map.120 = (f32[1024,512]{1,0:T(8,128)S(1)}, f32[1024,512]{1,0:T(8,128)S(1)}, bf16[1024,512]{1,0:T(8,128)(2,1)S(1)}) custom-call(bf16[2,1024,512]{2,1,0:T(8,128)(2,1)S(1)} %bitcast.18, bf16[1024,1024]{1,0:T(8,128)(2,1)S(1)} %get-tuple-element.17.basis, bf16[512,512]{1,0:T(8,128)(2,1)S(1)} %copy-done.8, f32[1024,512]{1,0:T(8,128)S(1)} %get-tuple-element.18.first, ...), custom_call_target="tpu_custom_call" | custom-call | flops 3221225472 | bytes 16777216 | tf_op jit(solution)/shard_map/pallas_call | solution.py:327
  86.0 0.0 copy-start.7
  86.0 1.1 constant_dynamic-slice_fusion
  87.1 0.9 collective-permute-start.3
  88.0 1.0 constant_dynamic-slice_fusion.1
  89.1 41.5 %shard_map.121 = (bf16[1024,1024]{1,0:T(8,128)(2,1)S(1)}, bf16[512,512]{1,0:T(8,128)(2,1)}) custom-call(bf16[2,1024,512]{2,1,0:T(8,128)(2,1)S(1)} %bitcast.19, f32[1024,1024]{1,0:T(8,128)} %get-tuple-element.22.stat, bf16[1024,1024]{1,0:T(8,128)(2,1)} %copy-done.5, f32[512,512]{1,0:T(8,128)S(1)} %copy-done.7, bf16[512,512]{1,0:T(8,128)(2,1)S(1)} %copy-done.8), custom_call_target="tpu_custom_call" | custom-call | flops 27917287424 | bytes 16777216 | tf_op jit(solution)/shard_map/pallas_call | solution.py:407
  130.6 1.3 copy-done.1
  131.9 1.0 constant_dynamic-slice_fusion.2
  132.9 0.5 collective-permute-start.1
  133.4 0.0 collective-permute-start
  133.4 1.8 %select_bitcast_fusion.1 = (f32[1,512,512]{2,1,0:T(8,128)S(1)}, f32[1,512,512]{2,1,0:T(8,128)S(1)}) fusion(f32[512,512]{1,0:T(8,128)} %collective-permute-done.3, f32[1024,512]{1,0:T(8,128)} %copy-done.3, s32[]{:T(128)S(6)} %select_n.58, pred[]{:T(512)S(6)} %eq.2), kind=kLoop, calls=%fused_computation.5 | loop fusion | flops 524288 | bytes 4194309 | tf_op jit(solution)/shard_map/stack | solution.py:446
  135.2 1.5 %pad_maximum_fusion.3 = f32[2,512,512]{2,1,0:T(8,128)} fusion(f32[1,512,512]{2,1,0:T(8,128)S(1)} %get-tuple-element.28, f32[1,512,512]{2,1,0:T(8,128)S(1)} %get-tuple-element.27), kind=kLoop, calls=%fused_computation.3 | loop fusion | flops 524288 | bytes 4194304 | tf_op jit(solution)/shard_map/stack | solution.py:446
  136.7 1.4 select_bitcast_fusion.3
  138.2 1.5 %pad_maximum_fusion.2 = f32[2,512,512]{2,1,0:T(8,128)} fusion(f32[1,512,512]{2,1,0:T(8,128)S(1)} %get-tuple-element.30, f32[1,512,512]{2,1,0:T(8,128)S(1)} %get-tuple-element.29), kind=kLoop, calls=%fused_computation.2 | loop fusion | flops 524288 | bytes 4194304 | tf_op jit(solution)/shard_map/stack | solution.py:446
  139.7 0.8 copy-done.2
  140.5 1.8 %select_bitcast_fusion.5 = (bf16[1,512,1024]{2,1,0:T(8,128)(2,1)S(1)}, bf16[1,512,1024]{2,1,0:T(8,128)(2,1)S(1)}) fusion(bf16[512,1024]{1,0:T(8,128)(2,1)} %collective-permute-done.1, pred[]{:T(512)S(6)} %eq.2, bf16[1024,1024]{1,0:T(8,128)(2,1)S(1)} %copy-done.2, s32[]{:T(128)S(6)} %select_n.58), kind=kLoop, calls=%fused_computation.9 | loop fusion | flops 1048576 | bytes 4194309 | tf_op jit(solution)/shard_map/stack | solution.py:446
  142.3 1.5 %pad_maximum_fusion.1 = bf16[2,512,1024]{2,1,0:T(8,128)(2,1)} fusion(bf16[1,512,1024]{2,1,0:T(8,128)(2,1)S(1)} %get-tuple-element.32, bf16[1,512,1024]{2,1,0:T(8,128)(2,1)S(1)} %get-tuple-element.31), kind=kLoop, calls=%fused_computation.1 | loop fusion | flops 1048576 | bytes 4194304 | tf_op jit(solution)/shard_map/stack | solution.py:446
  143.8 1.4 select_bitcast_fusion.7
  145.2 1.5 %pad_maximum_fusion = bf16[2,1024,512]{2,1,0:T(8,128)(2,1)} fusion(bf16[1,1024,512]{2,1,0:T(8,128)(2,1)S(1)} %get-tuple-element.34, bf16[1,1024,512]{2,1,0:T(8,128)(2,1)S(1)} %get-tuple-element.33), kind=kLoop, calls=%fused_computation | loop fusion | flops 1048576 | bytes 4194304 | tf_op jit(solution)/shard_map/stack | solution.py:446
  (16 shorter events, 0.0 us)
Async XLA Ops:
  0.6 1.6 %copy-start = (bf16[2,512,1024]{2,1,0:T(8,128)(2,1)S(1)}, bf16[2,512,1024]{2,1,0:T(8,128)(2,1)}, u32[]{:S(2)}) copy-start(bf16[2,512,1024]{2,1,0:T(8,128)(2,1)} %basis.1) | copy-start | bytes 6291460
  2.2 1.2 copy-start.4
  3.5 74.0 %copy-start.8 = (bf16[512,512]{1,0:T(8,128)(2,1)S(1)}, bf16[512,512]{1,0:T(8,128)(2,1)}, u32[]{:S(2)}) copy-start(bf16[512,512]{1,0:T(8,128)(2,1)} %right.3) | copy-start | bytes 1572868
  76.2 1.3 copy-start.6
  77.5 8.5 %copy-start.5 = (bf16[1024,1024]{1,0:T(8,128)(2,1)}, bf16[1024,1024]{1,0:T(8,128)(2,1)S(1)}, u32[]{:S(2)}) copy-start(bf16[1024,1024]{1,0:T(8,128)(2,1)S(1)} %get-tuple-element.17.basis) | copy-start | bytes 6291460
  86.0 3.1 %copy-start.3 = (f32[1024,512]{1,0:T(8,128)}, f32[1024,512]{1,0:T(8,128)S(1)}, u32[]{:S(2)}) copy-start(f32[1024,512]{1,0:T(8,128)S(1)} %get-tuple-element.26) | copy-start | bytes 6291460
  86.0 3.1 %copy-start.7 = (f32[512,512]{1,0:T(8,128)S(1)}, f32[512,512]{1,0:T(8,128)}, u32[]{:S(2)}) copy-start(f32[512,512]{1,0:T(8,128)} %stat_right.1) | copy-start | bytes 3145732
  87.1 46.3 %collective-permute-start.3 = (f32[512,512]{1,0:T(8,128)}, f32[512,512]{1,0:T(8,128)}, u32[]{:S(2)}, u32[]{:S(2)}) collective-permute-start(f32[512,512]{1,0:T(8,128)} %constant_dynamic-slice_fusion), channel_id=1, source_target_pairs={{0,1},{1,0},{2,3},{3,2},{4,5},{5,4},{6,7},{7,6},{8,9},{9,8},{10,11... | collective-permute-start | bytes 3145736 | tf_op jit(solution)/shard_map/ppermute | solution.py:440
  89.1 47.6 %collective-permute-start.2 = (f32[512,512]{1,0:T(8,128)}, f32[512,512]{1,0:T(8,128)}, u32[]{:S(2)}, u32[]{:S(2)}) collective-permute-start(f32[512,512]{1,0:T(8,128)} %constant_dynamic-slice_fusion.1), channel_id=1, source_target_pairs={{0,1},{1,0},{2,3},{3,2},{4,5},{5,4},{6,7},{7,6},{8,9},{9,8},{10,11... | collective-permute-start | bytes 3145736 | tf_op jit(solution)/shard_map/ppermute | solution.py:440
  130.6 1.3 copy-start.1
  132.9 6.8 %collective-permute-start.1 = (bf16[512,1024]{1,0:T(8,128)(2,1)}, bf16[512,1024]{1,0:T(8,128)(2,1)}, u32[]{:S(2)}, u32[]{:S(2)}) collective-permute-start(bf16[512,1024]{1,0:T(8,128)(2,1)} %constant_dynamic-slice_fusion.2), channel_id=1, source_target_pairs={{0,1},{1,0},{2,3},{3,2},{4,5},{5,4},{6,7},{7,6},{8,9},{9,8},{10,11... | collective-permute-start | bytes 3145736 | tf_op jit(solution)/shard_map/ppermute | solution.py:440
  133.4 10.4 %collective-permute-start = (bf16[1024,512]{1,0:T(8,128)(2,1)S(1)}, bf16[1024,512]{1,0:T(8,128)(2,1)}, u32[]{:S(2)}, u32[]{:S(2)}) collective-permute-start(bf16[1024,512]{1,0:T(8,128)(2,1)S(1)} %get-tuple-element.21), channel_id=1, source_target_pairs={{0,1},{1,0},{2,3},{3,2},{4,5},{5,4},{6,7},{7,6},{8,9},{9,8},{10,11... | collective-permute-start | bytes 3145736 | tf_op jit(solution)/shard_map/ppermute | solution.py:450
  138.2 2.4 %copy-start.2 = (bf16[1024,1024]{1,0:T(8,128)(2,1)S(1)}, bf16[1024,1024]{1,0:T(8,128)(2,1)}, u32[]{:S(2)}) copy-start(bf16[1024,1024]{1,0:T(8,128)(2,1)} %copy-done.1) | copy-start | bytes 6291460

commit v2 on v0

--- a/solution.py
+++ b/solution.py
@@ -1,6 +1,10 @@
+import functools
+
 import jax
 import jax.numpy as jnp
 from jax import lax
+from jax.experimental import pallas as pl
+from jax.experimental.pallas import tpu as pltpu
 from jax.sharding import PartitionSpec as P
 
 NS_ITERS = 3
@@ -118,7 +122,322 @@
     return (weights_new, basis_left_new, basis_right_new, moment_new, square_new)
 
 
+MESH = pl.DeviceIdType.MESH
+PLANE = 4
+LINE = 4
+ORDER = (2, 1, 3, 0)
+F32 = jnp.float32
+BF16 = jnp.bfloat16
+
+
+def dot(a, b, dims=((1,), (0,))):
+    return lax.dot_general(a, b, (dims, ((), ())), preferred_element_type=F32)
+
+
+def tile_rows(at, tile):
+    return pl.ds(pl.multiple_of(at * tile, tile), tile)
+
+
+def schulz_sweeps(start, gram, spare, size, tile):
+    chain = (start, spare, start, spare)
+    for sweep in range(NS_ITERS):
+        now, later = chain[sweep % 2], chain[sweep % 2 + 1]
+
+        @pl.loop(0, size // tile)
+        def _(at):
+            rows = tile_rows(at, tile)
+            gram[rows, :] = dot(now[rows, :], now[...], ((1,), (1,))).astype(BF16)
+
+        @pl.loop(0, size // tile)
+        def _(at):
+            rows = tile_rows(at, tile)
+            poly = schulz_cubic * gram[rows, :].astype(F32) + schulz_quintic * dot(gram[rows, :], gram[...])
+            later[rows, :] = (
+                schulz_linear * now[rows, :].astype(F32) + dot(poly.astype(BF16), now[...])
+            ).astype(BF16)
+    return later
+
+
+def step_kernel(
+    parts, weights_in, stat_in, stat_right, basis_in, right, first_in, second_in,
+    weights_out, basis_out, right_out, first_out, second_out,
+    far_part, near_part, pair_send, pair_recv, chip_low, plane_recv, line_send, line_recv,
+    grad, basis, stat, first, second, weights,
+    power, rot, half, start, spare, gram, rpower, rstart, rspare, rgram,
+    load_sem, pair_sem, plane_sem, line_sem, gline_sem, gplane_sem, gpair_sem, swap_sem, keep_sem,
+    give_sem, store_sem,
+):
+    rep = lax.axis_index("rep")
+    core = lax.axis_index("shard")
+    other = 1 - core
+    layer = rep // PLANE
+    spot = lax.rem(rep, PLANE)
+    size = basis.shape[0]
+    height = basis_in.shape[1]
+    piece = size // (PLANE * LINE)
+    tile = 256
+
+    def line_of(k):
+        return lax.rem(layer + k, LINE)
+
+    def spot_of(j):
+        return lax.rem(spot + j, PLANE)
+
+    def rows_of(p, z):
+        return pl.ds(pl.multiple_of((p * LINE + z) * piece, piece), piece)
+
+    loads = {}
+    for k in ORDER:
+        far = pltpu.make_async_copy(parts.at[other, :, line_of(k)], far_part.at[k], load_sem.at[0, k])
+        far.start()
+        near = pltpu.make_async_copy(parts.at[core, :, line_of(k)], near_part.at[k], load_sem.at[1, k])
+        near.start()
+        loads[k] = (far, near)
+    mine = pl.ds(pl.multiple_of(core * height, height), height)
+    theirs = pl.ds(pl.multiple_of(other * height, height), height)
+    moved = ((stat_in, stat), (basis_in, basis), (first_in, first), (second_in, second), (weights_in, weights))
+    keeps = []
+    for at, (source, target) in enumerate(moved):
+        keep = pltpu.make_async_copy(source.at[core], target.at[mine], keep_sem.at[at])
+        keep.start()
+        keeps.append(keep)
+
+    barrier = pltpu.get_barrier_semaphore()
+    partners = [(rep, other)]
+    partners += [(layer * PLANE + spot_of(j), core) for j in range(1, PLANE)]
+    partners += [(line_of(k) * PLANE + spot, core) for k in range(1, LINE)]
+    for partner in partners:
+        pl.semaphore_signal(barrier, inc=1, device_id=partner, device_id_type=MESH)
+    pl.semaphore_wait(barrier, len(partners))
+
+    def send(source, target, sems, partner):
+        copy = pltpu.make_async_remote_copy(
+            src_ref=source, dst_ref=target, send_sem=sems.at[0], recv_sem=sems.at[1],
+            device_id=partner, device_id_type=MESH,
+        )
+        copy.start()
+        return copy
+
+    pairs = {}
+    for k in ORDER:
+        loads[k][0].wait()
+        pair_send[k] = far_part[k].astype(BF16)
+        pairs[k] = send(pair_send.at[k], pair_recv.at[k], pair_sem.at[k], (rep, other))
+
+    planes = {}
+    for k in ORDER:
+        loads[k][1].wait()
+        pairs[k].wait_recv()
+        near_part[k] = near_part[k] + pair_recv[k].astype(F32)
+        chip_low[k] = near_part[k].astype(BF16)
+        for j in (2, 1, 3):
+            planes[k, j] = send(
+                chip_low.at[k, spot_of(j)], plane_recv.at[k, j - 1], plane_sem.at[k, j - 1],
+                (layer * PLANE + spot_of(j), core),
+            )
+
+    swaps = []
+    for at, (source, target) in enumerate(moved):
+        swaps.append(send(source.at[other], target.at[mine], swap_sem.at[at], (rep, other)))
+
+    lines = {}
+    total = None
+    for k in ORDER:
+        for j in range(1, PLANE):
+            planes[k, j].wait_recv()
+        total = near_part[k, spot]
+        for j in range(1, PLANE):
+            total = total + plane_recv[k, j - 1].astype(F32)
+        if k:
+            line_send[k - 1] = total.astype(BF16)
+            lines[k] = send(
+                line_send.at[k - 1], line_recv.at[k - 1], line_sem.at[k - 1],
+                (line_of(k) * PLANE + spot, core),
+            )
+    for k in range(1, LINE):
+        lines[k].wait_recv()
+        total = total + line_recv[k - 1].astype(F32)
+    own = rows_of(spot, layer)
+    grad[core, own, :] = (total * (1.0 / (PLANE * LINE))).astype(BF16)
+
+    def share(rows, sems, partner):
+        return send(grad.at[core, rows], grad.at[core, rows], sems, partner)
+
+    glines = {k: share(own, gline_sem.at[k - 1], (line_of(k) * PLANE + spot, core)) for k in (2, 1, 3)}
+    gplanes = {}
+    gpairs = []
+    for at, k in enumerate((0, 1, 3, 2)):
+        rows = rows_of(spot, lax.rem(layer + LINE - k, LINE))
+        if k:
+            glines[k].wait_recv()
+        for j in (2, 1, 3):
+            gplanes[k, j] = share(rows, gplane_sem.at[k, j - 1], (layer * PLANE + spot_of(j), core))
+        gpairs.append(share(rows, gpair_sem.at[k, 0], (rep, other)))
+        if at == 0:
+            for step in (0, 1):
+                swaps[step].wait_recv()
+                keeps[step].wait()
+        rows = pl.ds(at * (size // LINE), size // LINE)
+        power[rows, :] = stat_beta * dot(stat[rows, :].astype(BF16), basis[...])
+    for k in (0, 1, 3, 2):
+        for j in (1, 3, 2):
+            gplanes[k, j].wait_recv()
+            rows = rows_of(lax.rem(spot + PLANE - j, PLANE), lax.rem(layer + LINE - k, LINE))
+            gpairs.append(share(rows, gpair_sem.at[k, j], (rep, other)))
+    for step in (2, 3, 4):
+        swaps[step].wait_recv()
+        keeps[step].wait()
+
+    @pl.loop(0, size // tile)
+    def _(at):
+        rows = tile_rows(at, tile)
+        turned = dot(basis[:, rows], grad[core], ((0,), (0,))).astype(BF16)
+        rot[rows, :] = turned
+        rotated = dot(turned, right[...])
+        moment = moment_decay * first[rows, :] + (1.0 - moment_decay) * rotated
+        square = square_decay * second[rows, :] + (1.0 - square_decay) * rotated * rotated
+        first[rows, :] = moment
+        second[rows, :] = square
+        direction = moment / (jnp.sqrt(square) + epsilon)
+        half[rows, :] = dot(direction.astype(BF16), right[...], ((1,), (1,))).astype(BF16)
+
+    @pl.loop(0, size // tile)
+    def _(at):
+        rows = tile_rows(at, tile)
+        update = dot(basis[rows, :], half[...])
+        weights[rows, :] = (weights[rows, :].astype(F32) - learn_rate * update).astype(BF16)
+
+    gives = []
+    stores = []
+
+    def store(source, target):
+        copy = pltpu.make_async_copy(source, target, store_sem.at[len(stores)])
+        copy.start()
+        stores.append(copy)
+
+    def give(source, target):
+        gives.append(send(source, target, give_sem.at[len(gives)], (rep, other)))
+
+    give(weights, weights_out.at[core])
+    give(first.at[theirs], first_out.at[core])
+    give(second.at[theirs], second_out.at[core])
+    store(weights, weights_out.at[core])
+    store(first.at[mine], first_out.at[core])
+    store(second.at[mine], second_out.at[core])
+
+    def left_tile(at, squares):
+        rows = tile_rows(at, tile)
+        value = power[rows, :] + (1.0 - stat_beta) * dot(grad[core, rows, :], rot[...], ((1,), (1,)))
+        power[rows, :] = value
+        return squares + jnp.sum(value * value)
+
+    squares = lax.fori_loop(0, size // tile, left_tile, jnp.float32(0.0))
+    scale = lax.rsqrt(squares + norm_epsilon)
+
+    @pl.loop(0, size // tile)
+    def _(at):
+        rows = tile_rows(at, tile)
+        start[rows, :] = (power[rows, :] * scale).astype(BF16)
+
+    left = schulz_sweeps(start, gram, spare, size, 512)
+    give(left.at[theirs], basis_out.at[core])
+    store(left.at[mine], basis_out.at[core])
+
+    for copy in gpairs:
+        copy.wait_recv()
+    width = right.shape[0]
+
+    def right_tile(at, squares):
+        rows = tile_rows(at, tile)
+        terms = dot(grad[0, :, rows], grad[0], ((0,), (0,))) + dot(grad[1, :, rows], grad[1], ((0,), (0,)))
+        mixed = stat_beta * stat_right[rows, :] + (1.0 - stat_beta) * terms
+        value = dot(mixed.astype(BF16), right[...])
+        rpower[rows, :] = value
+        return squares + jnp.sum(value * value)
+
+    rsquares = lax.fori_loop(0, width // tile, right_tile, jnp.float32(0.0))
+    rscale = lax.rsqrt(rsquares + norm_epsilon)
+    rstart[...] = (rpower[...] * rscale).astype(BF16)
+    right_out[...] = schulz_sweeps(rstart, rgram, rspare, width, 512)[...]
+
+    for copy in gives:
+        copy.wait_recv()
+    for group in (pairs, planes, lines, glines, gplanes):
+        for copy in group.values():
+            copy.wait_send()
+    for copy in gpairs + swaps + gives:
+        copy.wait_send()
+    for copy in stores:
+        copy.wait()
+
+
+def on_device_blocks(
+    grad_parts, weights, stat_left, stat_right, basis_left, basis_right, moment_first, moment_second
+):
+    blocks, height, width = weights.shape
+    size = blocks * height
+    piece = size // (PLANE * LINE)
+    parts = grad_parts.reshape(blocks, PLANE, LINE, piece, width)
+    anywhere = pl.BlockSpec(memory_space=pl.ANY)
+    in_vmem = pl.BlockSpec(memory_space=pltpu.VMEM)
+    dma = pltpu.SemaphoreType.DMA
+    return pl.pallas_call(
+        step_kernel,
+        out_shape=(
+            jax.ShapeDtypeStruct((blocks, size, width), BF16),
+            jax.ShapeDtypeStruct((blocks, height, size), BF16),
+            jax.ShapeDtypeStruct((width, width), BF16),
+            jax.ShapeDtypeStruct((blocks, height, width), F32),
+            jax.ShapeDtypeStruct((blocks, height, width), F32),
+        ),
+        in_specs=[anywhere, anywhere, anywhere, in_vmem, anywhere, in_vmem, anywhere, anywhere],
+        out_specs=(anywhere, anywhere, in_vmem, anywhere, anywhere),
+        scratch_shapes=[
+            pltpu.VMEM((LINE, PLANE, piece, width), F32),
+            pltpu.VMEM((LINE, PLANE, piece, width), F32),
+            pltpu.VMEM((LINE, PLANE, piece, width), BF16),
+            pltpu.VMEM((LINE, PLANE, piece, width), BF16),
+            pltpu.VMEM((LINE, PLANE, piece, width), BF16),
+            pltpu.VMEM((LINE, PLANE - 1, piece, width), BF16),
+            pltpu.VMEM((LINE - 1, piece, width), BF16),
+            pltpu.VMEM((LINE - 1, piece, width), BF16),
+            pltpu.VMEM((blocks, size, width), BF16),
+            pltpu.VMEM((size, size), BF16),
+            pltpu.VMEM((size, size), F32),
+            pltpu.VMEM((size, width), F32),
+            pltpu.VMEM((size, width), F32),
+            pltpu.VMEM((size, width), BF16),
+            pltpu.VMEM((size, size), F32),
+            pltpu.VMEM((size, width), BF16),
+            pltpu.VMEM((size, width), BF16),
+            pltpu.VMEM((size, size), BF16),
+            pltpu.VMEM((size, size), BF16),
+            pltpu.VMEM((size, size), BF16),
+            pltpu.VMEM((width, width), F32),
+            pltpu.VMEM((width, width), BF16),
+            pltpu.VMEM((width, width), BF16),
+            pltpu.VMEM((width, width), BF16),
+            dma((2, LINE)),
+            dma((LINE, 2)),
+            dma((LINE, PLANE - 1, 2)),
+            dma((LINE - 1, 2)),
+            dma((LINE - 1, 2)),
+            dma((LINE, PLANE - 1, 2)),
+            dma((LINE, PLANE, 2)),
+            dma((5, 2)),
+            dma((5,)),
+            dma((4, 2)),
+            dma((4,)),
+        ],
+        compiler_params=pltpu.CompilerParams(
+            collective_id=0, has_side_effects=True, vmem_limit_bytes=60 << 20
+        ),
+    )(parts, weights, stat_left, stat_right, basis_left, basis_right, moment_first, moment_second)
+
+
 def solution(mesh):
+    fits = mesh.shape["shard"] == 2 and mesh.shape["rep"] == 16
+    body = on_device_blocks if fits else on_device
     placed = (
         P("rep", "shard", None, None, None),
         P(None, "shard", None),
@@ -130,7 +449,7 @@
         P(None, "shard", None),
     )
     return jax.shard_map(
-        on_device,
+        body,
         mesh=mesh,
         in_specs=placed,
         out_specs=(

time: 369 us -> 89 us (0.24)
  waiting for transfers between devices: 246 us -> 0 us
  matrix products: 88.6 us -> 0 us
  Pallas kernels: 0 us -> 78.5 us
  between operations: 16.6 us -> 0.66 us
  other arithmetic: 6.91 us -> 0 us
    psum x2 -> x0, waiting for transfers between devices: 166 us -> none  [the longest x1 150 us: on_device(): grad_total = lax.psum(partial_value, ('rep', 'shard')) / rep_count]
    dot_general x19 -> x0, matrix products: 88.6 us -> none  [the longest x3 32.7 us: schulz_split(): jnp.einsum('bij,bjk->bik', poly_rows, gathered, preferred_element_type=jn...]
    pallas_call x0 -> x1, Pallas kernels: none -> 78.5 us  [on_device_blocks(): pl.pallas_call(step_kernel, out_shape=(jax.ShapeDtypeStruct((blocks, size...]
    all_gather x9 -> x0, waiting for transfers between devices: 70.5 us -> none  [the longest x3 35.2 us: schulz_split(): gram_block = lax.all_gather(gram_rows, 'shard', axis=1, tiled=True)]
    reduce_scatter x1 -> x0, waiting for transfers between devices: 7.67 us -> none  [on_device(): lax.psum_scatter(local_turn.astype(jnp.bfloat16), 'shard', scatter_dimens...]
    convert_element_type x2 -> x0, other arithmetic: 6.9 us -> none  [the longest x1 4.14 us: on_device(): (power_rows * lax.rsqrt(block_squares + norm_epsilon)[:, None, None]).ast...]
    unnamed x16 -> x13, local copies, waits for them, and re-layouts: 6.25 us -> 9.57 us
  transfers between devices with their start and end apart: 12 -> 0, of which waited for: 10 -> 0; matrix products, arithmetic and copies ran while one was open for 17% -> 0% of each run, Pallas kernels for 0% -> 0%
where the time goes in v2:
time: 89 us; the launch traced here: 88.8 us
  Pallas kernels  78.5 us (88%)
  local copies, waits for them, and re-layouts  9.57 us (11%)
    pallas_call x1, Pallas kernels, on_device_blocks(): pl.pallas_call(step_kernel, out_shape=(jax.ShapeDtypeStruct((blocks, size...  78.5 us
    unnamed x13, local copies, waits for them, and re-layouts  9.57 us

profile of v2, /device:TPU:0, one launch (start us, length us, event | category | flops | bytes accessed | tf_op | source)
XLA Modules:
  0.0 88.8 jit_solution(18311738845952698505)
XLA Ops:
  0.6 78.5 %shard_map.119 = (bf16[2,1024,512]{2,1,0:T(8,128)(2,1)}, bf16[2,512,1024]{2,1,0:T(8,128)(2,1)}, bf16[512,512]{1,0:T(8,128)(2,1)}, f32[2,512,512]{2,1,0:T(8,128)}, f32[2,512,512]{2,1,0:T(8,128)}) custom-call(f32[2,4,4,64,512]{4,3,2,1,0:T(8,128)} %bitcast.1, bf16[2,512,512]{2,1,0:T(8,128)(2,1)} %weights_in.1, f32[2,512,1024]{2,1,0:T(8,128)} %stat_in.1, ...), custom_call_target="tpu_custom_call" | custom-call | tf_op jit(solution)/shard_map/pallas_call | solution.py:384
  79.2 0.0 copy-start.2
  79.2 3.2 %copy.18 = bf16[2,1024,512]{2,1,0:T(8,128)(2,1)} copy(bf16[2,1024,512]{2,1,0:T(8,128)(2,1)} %get-tuple-element.10) | data formatting | bytes 4194304
  82.4 0.0 copy-done.2
  82.4 0.0 copy-start.3
  82.4 0.0 copy-start.1
  82.4 1.3 %copy.19 = bf16[2,512,1024]{2,1,0:T(8,128)(2,1)} copy(bf16[2,512,1024]{2,1,0:T(8,128)(2,1)S(1)} %copy-done.2) | data formatting | bytes 4194304
  83.7 0.1 copy-done.3
  83.8 0.8 copy.20
  84.6 0.5 copy-done.1
  85.1 0.0 copy-start
  85.1 1.3 %copy.21 = f32[2,512,512]{2,1,0:T(8,128)} copy(f32[2,512,512]{2,1,0:T(8,128)S(1)} %copy-done.1) | data formatting | bytes 4194304
  86.4 1.0 %copy-done = f32[2,512,512]{2,1,0:T(8,128)S(1)} copy-done((f32[2,512,512]{2,1,0:T(8,128)S(1)}, f32[2,512,512]{2,1,0:T(8,128)}, u32[]{:S(2)}) %copy-start) | copy-done | bytes 2097176
  87.4 1.3 %copy.22 = f32[2,512,512]{2,1,0:T(8,128)} copy(f32[2,512,512]{2,1,0:T(8,128)S(1)} %copy-done) | data formatting | bytes 4194304
Async XLA Ops:
  79.2 3.2 %copy-start.2 = (bf16[2,512,1024]{2,1,0:T(8,128)(2,1)S(1)}, bf16[2,512,1024]{2,1,0:T(8,128)(2,1)}, u32[]{:S(2)}) copy-start(bf16[2,512,1024]{2,1,0:T(8,128)(2,1)} %get-tuple-element.11) | copy-start | bytes 6291460
  82.4 1.4 %copy-start.3 = (bf16[512,512]{1,0:T(8,128)(2,1)S(1)}, bf16[512,512]{1,0:T(8,128)(2,1)}, u32[]{:S(2)}) copy-start(bf16[512,512]{1,0:T(8,128)(2,1)} %get-tuple-element.12) | copy-start | bytes 1572868
  82.4 2.7 %copy-start.1 = (f32[2,512,512]{2,1,0:T(8,128)S(1)}, f32[2,512,512]{2,1,0:T(8,128)}, u32[]{:S(2)}) copy-start(f32[2,512,512]{2,1,0:T(8,128)} %get-tuple-element.13) | copy-start | bytes 6291460
  85.1 2.3 %copy-start = (f32[2,512,512]{2,1,0:T(8,128)S(1)}, f32[2,512,512]{2,1,0:T(8,128)}, u32[]{:S(2)}) copy-start(f32[2,512,512]{2,1,0:T(8,128)} %get-tuple-element.14) | copy-start | bytes 6291460

commit v3 on v2

--- a/solution.py
+++ b/solution.py
@@ -163,7 +163,7 @@
     weights_out, basis_out, right_out, first_out, second_out,
     far_part, near_part, pair_send, pair_recv, chip_low, plane_recv, line_send, line_recv,
     grad, basis, stat, first, second, weights,
-    power, rot, half, start, spare, gram, rpower, rstart, rspare, rgram,
+    power, rot, rot_sum, half, start, spare, gram, rpower, rterm,
     load_sem, pair_sem, plane_sem, line_sem, gline_sem, gplane_sem, gpair_sem, swap_sem, keep_sem,
     give_sem, store_sem,
 ):
@@ -184,13 +184,13 @@
         return lax.rem(spot + j, PLANE)
 
     def rows_of(p, z):
-        return pl.ds(pl.multiple_of((p * LINE + z) * piece, piece), piece)
+        return pl.ds(pl.multiple_of((z * PLANE + p) * piece, piece), piece)
 
     loads = {}
     for k in ORDER:
-        far = pltpu.make_async_copy(parts.at[other, :, line_of(k)], far_part.at[k], load_sem.at[0, k])
+        far = pltpu.make_async_copy(parts.at[other, line_of(k)], far_part.at[k], load_sem.at[0, k])
         far.start()
-        near = pltpu.make_async_copy(parts.at[core, :, line_of(k)], near_part.at[k], load_sem.at[1, k])
+        near = pltpu.make_async_copy(parts.at[core, line_of(k)], near_part.at[k], load_sem.at[1, k])
         near.start()
         loads[k] = (far, near)
     mine = pl.ds(pl.multiple_of(core * height, height), height)
@@ -284,6 +284,20 @@
             gplanes[k, j].wait_recv()
             rows = rows_of(lax.rem(spot + PLANE - j, PLANE), lax.rem(layer + LINE - k, LINE))
             gpairs.append(share(rows, gpair_sem.at[k, j], (rep, other)))
+        group = tile_rows(lax.rem(layer + LINE - k, LINE), size // LINE)
+        if k == 0:
+            rterm[...] = dot(grad[core, group, :], grad[core, group, :], ((0,), (0,)))
+        else:
+            rterm[...] += dot(grad[core, group, :], grad[core, group, :], ((0,), (0,)))
+
+        @pl.loop(0, size // tile)
+        def _(at):
+            rows = tile_rows(at, tile)
+            added = dot(basis[group, rows], grad[core, group, :], ((0,), (0,)))
+            if k == 0:
+                rot_sum[rows, :] = added
+            else:
+                rot_sum[rows, :] += added
     for step in (2, 3, 4):
         swaps[step].wait_recv()
         keeps[step].wait()
@@ -291,7 +305,7 @@
     @pl.loop(0, size // tile)
     def _(at):
         rows = tile_rows(at, tile)
-        turned = dot(basis[:, rows], grad[core], ((0,), (0,))).astype(BF16)
+        turned = rot_sum[rows, :].astype(BF16)
         rot[rows, :] = turned
         rotated = dot(turned, right[...])
         moment = moment_decay * first[rows, :] + (1.0 - moment_decay) * rotated
@@ -339,7 +353,7 @@
         rows = tile_rows(at, tile)
         start[rows, :] = (power[rows, :] * scale).astype(BF16)
 
-    left = schulz_sweeps(start, gram, spare, size, 512)
+    left = schulz_sweeps(start, gram, spare, size, size)
     give(left.at[theirs], basis_out.at[core])
     store(left.at[mine], basis_out.at[core])
 
@@ -349,7 +363,7 @@
 
     def right_tile(at, squares):
         rows = tile_rows(at, tile)
-        terms = dot(grad[0, :, rows], grad[0], ((0,), (0,))) + dot(grad[1, :, rows], grad[1], ((0,), (0,)))
+        terms = rterm[rows, :] + dot(grad[other, :, rows], grad[other], ((0,), (0,)))
         mixed = stat_beta * stat_right[rows, :] + (1.0 - stat_beta) * terms
         value = dot(mixed.astype(BF16), right[...])
         rpower[rows, :] = value
@@ -357,8 +371,7 @@
 
     rsquares = lax.fori_loop(0, width // tile, right_tile, jnp.float32(0.0))
     rscale = lax.rsqrt(rsquares + norm_epsilon)
-    rstart[...] = (rpower[...] * rscale).astype(BF16)
-    right_out[...] = schulz_sweeps(rstart, rgram, rspare, width, 512)[...]
+    right_out[...] = (rpower[...] * rscale).astype(BF16)
 
     for copy in gives:
         copy.wait_recv()
@@ -371,17 +384,61 @@
         copy.wait()
 
 
+def finish_kernel(
+    start, weights, basis, first, second, right_out, weights_out, basis_out, first_out, second_out,
+    hold_weights, hold_basis, hold_first, hold_second, now, spare, gram, load_sem, store_sem,
+):
+    moves = (
+        (weights, hold_weights, weights_out),
+        (basis, hold_basis, basis_out),
+        (first, hold_first, first_out),
+        (second, hold_second, second_out),
+    )
+    loads = []
+    stores = []
+    for at, (source, hold, target) in enumerate(moves):
+        load = pltpu.make_async_copy(source, hold, load_sem.at[at])
+        load.start()
+        loads.append(load)
+    now[...] = start[...]
+    for at, (source, hold, target) in enumerate(moves):
+        loads[at].wait()
+        store = pltpu.make_async_copy(hold, target, store_sem.at[at])
+        store.start()
+        stores.append(store)
+    right_out[...] = schulz_sweeps(now, gram, spare, now.shape[0], now.shape[0])[...]
+    for store in stores:
+        store.wait()
+
+
+def finish_right(start, *held):
+    anywhere = pl.BlockSpec(memory_space=pl.ANY)
+    in_vmem = pl.BlockSpec(memory_space=pltpu.VMEM)
+    dma = pltpu.SemaphoreType.DMA
+    width = start.shape[0]
+    return pl.pallas_call(
+        finish_kernel,
+        out_shape=[jax.ShapeDtypeStruct(a.shape, a.dtype) for a in (start,) + held],
+        in_specs=[in_vmem] + [anywhere] * 4,
+        out_specs=[in_vmem] + [anywhere] * 4,
+        scratch_shapes=[pltpu.VMEM(a.shape, a.dtype) for a in held]
+        + [pltpu.VMEM((width, width), BF16)] * 3
+        + [dma((4,)), dma((4,))],
+        compiler_params=pltpu.CompilerParams(vmem_limit_bytes=62 << 20),
+    )(start, *held)
+
+
 def on_device_blocks(
     grad_parts, weights, stat_left, stat_right, basis_left, basis_right, moment_first, moment_second
 ):
     blocks, height, width = weights.shape
     size = blocks * height
     piece = size // (PLANE * LINE)
-    parts = grad_parts.reshape(blocks, PLANE, LINE, piece, width)
+    parts = grad_parts.reshape(blocks, LINE, PLANE, piece, width)
     anywhere = pl.BlockSpec(memory_space=pl.ANY)
     in_vmem = pl.BlockSpec(memory_space=pltpu.VMEM)
     dma = pltpu.SemaphoreType.DMA
-    return pl.pallas_call(
+    weights_new, left_new, right_start, first_new, second_new = pl.pallas_call(
         step_kernel,
         out_shape=(
             jax.ShapeDtypeStruct((blocks, size, width), BF16),
@@ -409,14 +466,13 @@
             pltpu.VMEM((size, width), BF16),
             pltpu.VMEM((size, size), F32),
             pltpu.VMEM((size, width), BF16),
+            pltpu.VMEM((size, width), F32),
             pltpu.VMEM((size, width), BF16),
             pltpu.VMEM((size, size), BF16),
             pltpu.VMEM((size, size), BF16),
             pltpu.VMEM((size, size), BF16),
             pltpu.VMEM((width, width), F32),
-            pltpu.VMEM((width, width), BF16),
-            pltpu.VMEM((width, width), BF16),
-            pltpu.VMEM((width, width), BF16),
+            pltpu.VMEM((width, width), F32),
             dma((2, LINE)),
             dma((LINE, 2)),
             dma((LINE, PLANE - 1, 2)),
@@ -433,6 +489,10 @@
             collective_id=0, has_side_effects=True, vmem_limit_bytes=60 << 20
         ),
     )(parts, weights, stat_left, stat_right, basis_left, basis_right, moment_first, moment_second)
+    right_new, weights_new, left_new, first_new, second_new = finish_right(
+        right_start, weights_new, left_new, first_new, second_new
+    )
+    return weights_new, left_new, right_new, first_new, second_new
 
 
 def solution(mesh):

time: 89 us -> 84.6 us (0.951)
  local copies, waits for them, and re-layouts: 9.57 us -> 0 us
  Pallas kernels: 78.5 us -> 83.6 us
    pallas_call x0 -> x1, Pallas kernels: none -> 10.5 us  [finish_right(): pl.pallas_call(finish_kernel, out_shape=[jax.ShapeDtypeStruct(a.shape, a....]
    unnamed x13 -> x0, local copies, waits for them, and re-layouts: 9.57 us -> none
    pallas_call x1, Pallas kernels: 78.5 us -> 73.1 us  [on_device_blocks(): pl.pallas_call(step_kernel, out_shape=(jax.ShapeDtypeStruct((blocks, size...]
where the time goes in v3:
time: 84.6 us; the launch traced here: 84.4 us
  Pallas kernels  83.6 us (99%)
    pallas_call x1, Pallas kernels, on_device_blocks(): pl.pallas_call(step_kernel, out_shape=(jax.ShapeDtypeStruct((blocks, size...  73.1 us
    pallas_call x1, Pallas kernels, finish_right(): pl.pallas_call(finish_kernel, out_shape=[jax.ShapeDtypeStruct(a.shape, a....  10.5 us

profile of v3, /device:TPU:0, one launch (start us, length us, event | category | flops | bytes accessed | tf_op | source)
XLA Modules:
  0.0 84.4 jit_solution(14155775954399984916)
XLA Ops:
  0.6 73.1 %shard_map.119 = (bf16[2,1024,512]{2,1,0:T(8,128)(2,1)}, bf16[2,512,1024]{2,1,0:T(8,128)(2,1)}, bf16[512,512]{1,0:T(8,128)(2,1)}, f32[2,512,512]{2,1,0:T(8,128)}, f32[2,512,512]{2,1,0:T(8,128)}) custom-call(f32[2,4,4,64,512]{4,3,2,1,0:T(8,128)} %bitcast.1, bf16[2,512,512]{2,1,0:T(8,128)(2,1)} %weights_in.1, f32[2,512,1024]{2,1,0:T(8,128)} %stat_in.1, ...), custom_call_target="tpu_custom_call" | custom-call | tf_op jit(solution)/shard_map/pallas_call | solution.py:441
  73.7 10.5 %shard_map.120 = (bf16[512,512]{1,0:T(8,128)(2,1)}, bf16[2,1024,512]{2,1,0:T(8,128)(2,1)}, bf16[2,512,1024]{2,1,0:T(8,128)(2,1)}, f32[2,512,512]{2,1,0:T(8,128)}, f32[2,512,512]{2,1,0:T(8,128)}) custom-call(bf16[512,512]{1,0:T(8,128)(2,1)} %get-tuple-element.15.start, bf16[2,1024,512]{2,1,0:T(8,128)(2,1)} %get-tuple-element.16.weights, ...), custom_call_target="tpu_custom_call" | custom-call | tf_op jit(solution)/shard_map/pallas_call | solution.py:419
